TPU v7x, 512 devices: a whole 4x4x16 slice. The times are simulated.
512 devices in a mesh: seq: 16 (over y, x), dp: 32 (over z, core).
Axes of the slice: x: 4, y: 4, z: 16, core: 2. Of those that a mesh axis runs over, the one named last changes fastest.
Arguments:
- queries: bfloat16 [32, 2048, 2048], P('dp', 'seq'), may hold values from -30 to 30
- key_states: bfloat16 [32, 2048, 2048], P('dp', 'seq'), may hold values from -4.5 to 4.5
- value_states: bfloat16 [32, 2048, 2048], P('dp', 'seq'), may hold values from -6 to 6
- grad_out: bfloat16 [32, 2048, 2048], P('dp', 'seq'), may hold values from -18 to 18
- out_weight: bfloat16 [2048, 2048], P('dp'), may hold values from -0.125 to 0.125
- block_lists: int32 [16, 16, 8], P('seq'), may hold values from 0 to 15, as said below
- block_counts: int32 [16, 16], P('seq'), may hold values from 1 to 8, as said below
Outputs:
- query_grad: bfloat16 [32, 2048, 2048], P('dp', 'seq')
- key_grad: bfloat16 [32, 2048, 2048], P('dp', 'seq')
- value_grad: bfloat16 [32, 2048, 2048], P('dp', 'seq')
Inputs may be any that keep to these rules, and one draw needn't show every extreme that they name: The entries of one row block_lists[h, i, :] are distinct. `block_counts`: the counts of one head sum to at most 64; in every draw some head sums to exactly 64 and some query block uses all 8 entries.
All inputs are finite; a program needn't handle non-finite values.
Results may differ from a plain program's by a relative error of at most 0.0093.
Values may be sent and summed in bfloat16 or wider, within the bound.
A program may use at most 64 MiB of HBM per device.

v0:
```python
import jax
import jax.numpy as jnp
from jax import lax
from jax.sharding import PartitionSpec as P

HD = 128


def whole_rows(query_blocks, key_blocks, value_blocks, grad_blocks, lists_head, counts_head):
    nblocks, block_rows, head_width = query_blocks.shape
    kslots = lists_head.shape[1]
    group = 4
    score_scale = head_width ** (-0.5)

    def scan_step(running, block_slot):
        key_sum, value_sum = running
        query_group, grad_group, lists_group, counts_group = block_slot
        key_sets = key_blocks[lists_group]
        value_sets = value_blocks[lists_group]
        live_slots = jnp.arange(kslots, dtype=jnp.int32)[None, :] < counts_group[:, None]
        live_mask = live_slots[:, None, :, None]
        scores = (
            jnp.einsum("gqd,gjkd->gqjk", query_group, key_sets, preferred_element_type=jnp.float32)
            * score_scale
        )
        scores = jnp.where(live_mask, scores, -1e30)
        row_top = jnp.max(scores, axis=(2, 3), keepdims=True)
        weights = jnp.where(live_mask, jnp.exp(scores - row_top), 0.0)
        attn_probs = weights / jnp.sum(weights, axis=(2, 3), keepdims=True)
        probs_low = attn_probs.astype(jnp.bfloat16)
        attn_out = jnp.einsum(
            "gqjk,gjkd->gqd", probs_low, value_sets, preferred_element_type=jnp.float32
        )
        row_delta = jnp.sum(grad_group.astype(jnp.float32) * attn_out, axis=-1)
        prob_grad = jnp.einsum(
            "gqd,gjkd->gqjk", grad_group, value_sets, preferred_element_type=jnp.float32
        )
        score_low = (attn_probs * (prob_grad - row_delta[:, :, None, None])).astype(jnp.bfloat16)
        query_part = (
            jnp.einsum("gqjk,gjkd->gqd", score_low, key_sets, preferred_element_type=jnp.float32)
            * score_scale
        )
        key_parts = jnp.einsum(
            "gqjk,gqd->gjkd", score_low, query_group, preferred_element_type=jnp.float32
        )
        value_parts = jnp.einsum(
            "gqjk,gqd->gjkd", probs_low, grad_group, preferred_element_type=jnp.float32
        )
        key_sum = key_sum.at[lists_group].add(key_parts)
        value_sum = value_sum.at[lists_group].add(value_parts)
        return ((key_sum, value_sum), query_part.astype(jnp.bfloat16))

    def grouped(array):
        return array.reshape((nblocks // group, group) + array.shape[1:])

    empty_sum = jnp.zeros(query_blocks.shape, jnp.float32)
    final_state, query_part = lax.scan(
        scan_step,
        (empty_sum, empty_sum),
        (grouped(query_blocks), grouped(grad_blocks), grouped(lists_head), grouped(counts_head)),
    )
    key_sum, value_sum = final_state
    return (
        query_part.reshape(query_blocks.shape),
        (key_sum * score_scale).astype(jnp.bfloat16),
        value_sum.astype(jnp.bfloat16),
    )


def local(queries, key_states, value_states, grad_out, out_weight, block_lists, block_counts):
    tok_rows = queries.shape[1]
    model_width = queries.shape[2]
    head_total = model_width // HD
    head_local, nblocks, kslots = block_lists.shape

    def split_heads(matrix):
        return matrix.reshape(tok_rows, head_total, HD)

    def to_blocks(matrix):
        return jnp.moveaxis(matrix, 1, 0).reshape(head_local, nblocks, -1, HD)

    def from_blocks(blocks):
        return jnp.moveaxis(blocks.reshape(head_local, -1, HD), 0, 1)

    query_heads, key_heads, value_heads = (
        lax.all_to_all(split_heads(queries), "seq", split_axis=1, concat_axis=0, tiled=True),
        lax.all_to_all(split_heads(key_states), "seq", split_axis=1, concat_axis=0, tiled=True),
        lax.all_to_all(split_heads(value_states), "seq", split_axis=1, concat_axis=0, tiled=True),
    )
    query_blocks = to_blocks(query_heads)
    key_blocks = to_blocks(key_heads)
    value_blocks = to_blocks(value_heads)
    grad_rows = grad_out.reshape(tok_rows, model_width)
    attn_full = lax.dot_general(
        grad_rows,
        lax.all_gather(out_weight, "dp", axis=0, tiled=True),
        (((1,), (1,)), ((), ())),
        preferred_element_type=jnp.float32,
    )
    attn_low = attn_full.astype(jnp.bfloat16)
    grad_heads = lax.all_to_all(
        split_heads(attn_low), "seq", split_axis=1, concat_axis=0, tiled=True
    )
    grad_blocks = to_blocks(grad_heads)
    query_part, key_part, value_part = jax.vmap(whole_rows)(
        query_blocks, key_blocks, value_blocks, grad_blocks, block_lists, block_counts
    )
    returned = (
        lax.all_to_all(from_blocks(query_part), "seq", split_axis=0, concat_axis=1, tiled=True),
        lax.all_to_all(from_blocks(key_part), "seq", split_axis=0, concat_axis=1, tiled=True),
        lax.all_to_all(from_blocks(value_part), "seq", split_axis=0, concat_axis=1, tiled=True),
    )
    return (
        returned[0].reshape(1, tok_rows, model_width),
        returned[1].reshape(1, tok_rows, model_width),
        returned[2].reshape(1, tok_rows, model_width),
    )


def solution(mesh):
    placed = (
        P("dp", "seq", None),
        P("dp", "seq", None),
        P("dp", "seq", None),
        P("dp", "seq", None),
        P("dp", None),
        P("seq", None, None),
        P("seq", None),
    )
    return jax.shard_map(
        local,
        mesh=mesh,
        in_specs=placed,
        out_specs=(P("dp", "seq", None), P("dp", "seq", None), P("dp", "seq", None)),
        check_vma=False,
    )
```

profile of v0, /device:TPU:1, one launch (start us, length us, event | category | flops | bytes accessed | tf_op | source)
XLA Modules:
  0.0 277.1 jit_solution(4677492128257543968)
XLA Ops:
  10.0 7.6 %all-to-all-start = ((bf16[128,16,128]{2,0,1:T(8,128)(2,1)}), bf16[128,16,128]{2,0,1:T(8,128)(2,1)}, u32[]{:S(2)}, u32[]{:S(2)}) async-start(bf16[128,16,128]{2,0,1:T(8,128)(2,1)} %copy.81), calls=%async_computation | async-start | bytes 1048576 | tf_op jit(solution)/shard_map/all_to_all | solution.py:86
  18.7 8.0 %all-to-all-done = bf16[128,16,128]{2,0,1:T(8,128)(2,1)} async-done(((bf16[128,16,128]{2,0,1:T(8,128)(2,1)}), bf16[128,16,128]{2,0,1:T(8,128)(2,1)}, u32[]{:S(2)}, u32[]{:S(2)}) %all-to-all-start) | async-done | bytes 524320 | tf_op jit(solution)/shard_map/all_to_all | solution.py:86
  26.7 3.6 %all-to-all-start.1 = ((bf16[128,16,128]{0,2,1:T(8,128)(2,1)}), bf16[128,16,128]{0,2,1:T(8,128)(2,1)S(1)}, u32[]{:S(2)}, u32[]{:S(2)}) async-start(bf16[128,16,128]{0,2,1:T(8,128)(2,1)} %bitcast.29), calls=%async_computation.1 | async-start | bytes 1048576 | tf_op jit(solution)/shard_map/all_to_all | solution.py:87
  31.3 8.0 %all-to-all-done.1 = bf16[128,16,128]{0,2,1:T(8,128)(2,1)S(1)} async-done(((bf16[128,16,128]{0,2,1:T(8,128)(2,1)}), bf16[128,16,128]{0,2,1:T(8,128)(2,1)S(1)}, u32[]{:S(2)}, u32[]{:S(2)}) %all-to-all-start.1) | async-done | bytes 524320 | tf_op jit(solution)/shard_map/all_to_all | solution.py:87
  39.3 3.6 %all-to-all-start.3 = ((bf16[128,16,128]{0,2,1:T(8,128)(2,1)}), bf16[128,16,128]{0,2,1:T(8,128)(2,1)S(1)}, u32[]{:S(2)}, u32[]{:S(2)}) async-start(bf16[128,16,128]{0,2,1:T(8,128)(2,1)} %bitcast.38), calls=%async_computation.3 | async-start | bytes 1048576 | tf_op jit(solution)/shard_map/all_to_all | solution.py:88
  42.8 51.7 %all-gather.2.cloned.1.call-done = bf16[2048,2048]{1,0:T(8,128)(2,1)} async-done(((bf16[64,2048]{1,0:T(8,128)(2,1)}), bf16[2048,2048]{1,0:T(8,128)(2,1)}) %all-gather.2.cloned.1.call-update) | async-done | bytes 8388624 | tf_op jit(solution)/shard_map/all_gather | solution.py:96
  94.6 6.3 %fusion.29 = bf16[16,16,8,128]{3,2,1,0:T(8,128)(2,1)S(1)} fusion(bf16[2048,2048]{1,0:T(8,128)(2,1)} %all-gather.2.cloned.1.call-done, bf16[1,128,2048]{2,1,0:T(8,128)(2,1)S(1)} %copy-done), kind=kOutput, calls=%fused_computation.43 | convolution fusion | flops 1074003968 | bytes 9437184 | tf_op jit(solution)/shard_map/dot_general | solution.py:94
  101.8 6.8 %all-to-all-start.2 = ((bf16[128,16,128]{2,0,1:T(8,128)(2,1)}), bf16[128,16,128]{2,0,1:T(8,128)(2,1)}, u32[]{:S(2)}, u32[]{:S(2)}) async-start(bf16[128,16,128]{2,0,1:T(8,128)(2,1)} %bitcast.120), calls=%async_computation.2 | async-start | bytes 1048576 | tf_op jit(solution)/shard_map/all_to_all | solution.py:101
  111.2 8.2 %all-to-all-done.2 = bf16[128,16,128]{2,0,1:T(8,128)(2,1)} async-done(((bf16[128,16,128]{2,0,1:T(8,128)(2,1)}), bf16[128,16,128]{2,0,1:T(8,128)(2,1)}, u32[]{:S(2)}, u32[]{:S(2)}) %all-to-all-start.2) | async-done | bytes 524320 | tf_op jit(solution)/shard_map/all_to_all | solution.py:101
  121.7 104.1 %while.14 = (s32[]{:T(128)}, f32[1,16,128,128]{3,2,1,0:T(8,128)}, f32[1,16,128,128]{3,2,1,0:T(8,128)}, bf16[4,1,4,128,128]{4,3,2,1,0:T(8,128)(2,1)}, s32[4,1,4,8...) while((s32[]{:T(128)}, f32[1,16,128,128]{3,2,1,0:T(8,128)}, ...), condition=%wide.region_6.7_spmd, body=%wide.region_0.6_spmd.sunk | while | flops 821361536 | bytes 47997756 | solution.py:57
  122.7 2.7 gather_fusion
  133.9 6.1 %scatter_fusion.1 = f32[16,128,128]{2,1,0:T(8,128)} fusion(f32[16,128,128]{2,1,0:T(8,128)} %bitcast.168, s32[32]{0:T(128)S(1)} %reshape.276, f32[32,128,128]{2,1,0:T(8,128)S(1)} %bitcast.174), kind=kCustom, calls=%fused_computation.3.clone.1 | custom fusion | flops 524288 | bytes 6291584 | tf_op jit(solution)/shard_map/vmap()/while/body/eval_jaxpr/scatter-add | solution.py:50
  141.6 6.1 %scatter_fusion = f32[16,128,128]{2,1,0:T(8,128)} fusion(f32[16,128,128]{2,1,0:T(8,128)} %bitcast.163, s32[32]{0:T(128)S(1)} %reshape.276, f32[32,128,128]{2,1,0:T(8,128)S(1)} %bitcast.173), kind=kCustom, calls=%fused_computation.2.clone.1 | custom fusion | flops 524288 | bytes 6291584 | tf_op jit(solution)/shard_map/vmap()/while/body/eval_jaxpr/scatter-add | solution.py:49
  148.7 2.7 gather_fusion
  153.5 1.8 fusion.70
  159.9 6.1 %scatter_fusion.1 = f32[16,128,128]{2,1,0:T(8,128)} fusion(f32[16,128,128]{2,1,0:T(8,128)} %bitcast.168, s32[32]{0:T(128)S(1)} %reshape.276, f32[32,128,128]{2,1,0:T(8,128)S(1)} %bitcast.174), kind=kCustom, calls=%fused_computation.3.clone.1 | custom fusion | flops 524288 | bytes 6291584 | tf_op jit(solution)/shard_map/vmap()/while/body/eval_jaxpr/scatter-add | solution.py:50
  167.6 6.1 %scatter_fusion = f32[16,128,128]{2,1,0:T(8,128)} fusion(f32[16,128,128]{2,1,0:T(8,128)} %bitcast.163, s32[32]{0:T(128)S(1)} %reshape.276, f32[32,128,128]{2,1,0:T(8,128)S(1)} %bitcast.173), kind=kCustom, calls=%fused_computation.2.clone.1 | custom fusion | flops 524288 | bytes 6291584 | tf_op jit(solution)/shard_map/vmap()/while/body/eval_jaxpr/scatter-add | solution.py:49
  174.7 2.7 gather_fusion
  179.6 1.8 fusion.70
  185.9 6.1 %scatter_fusion.1 = f32[16,128,128]{2,1,0:T(8,128)} fusion(f32[16,128,128]{2,1,0:T(8,128)} %bitcast.168, s32[32]{0:T(128)S(1)} %reshape.276, f32[32,128,128]{2,1,0:T(8,128)S(1)} %bitcast.174), kind=kCustom, calls=%fused_computation.3.clone.1 | custom fusion | flops 524288 | bytes 6291584 | tf_op jit(solution)/shard_map/vmap()/while/body/eval_jaxpr/scatter-add | solution.py:50
  193.6 6.1 %scatter_fusion = f32[16,128,128]{2,1,0:T(8,128)} fusion(f32[16,128,128]{2,1,0:T(8,128)} %bitcast.163, s32[32]{0:T(128)S(1)} %reshape.276, f32[32,128,128]{2,1,0:T(8,128)S(1)} %bitcast.173), kind=kCustom, calls=%fused_computation.2.clone.1 | custom fusion | flops 524288 | bytes 6291584 | tf_op jit(solution)/shard_map/vmap()/while/body/eval_jaxpr/scatter-add | solution.py:49
  200.8 2.7 gather_fusion
  205.6 1.8 fusion.70
  211.9 6.1 %scatter_fusion.1 = f32[16,128,128]{2,1,0:T(8,128)} fusion(f32[16,128,128]{2,1,0:T(8,128)} %bitcast.168, s32[32]{0:T(128)S(1)} %reshape.276, f32[32,128,128]{2,1,0:T(8,128)S(1)} %bitcast.174), kind=kCustom, calls=%fused_computation.3.clone.1 | custom fusion | flops 524288 | bytes 6291584 | tf_op jit(solution)/shard_map/vmap()/while/body/eval_jaxpr/scatter-add | solution.py:50
  219.7 6.1 %scatter_fusion = f32[16,128,128]{2,1,0:T(8,128)} fusion(f32[16,128,128]{2,1,0:T(8,128)} %bitcast.163, s32[32]{0:T(128)S(1)} %reshape.276, f32[32,128,128]{2,1,0:T(8,128)S(1)} %bitcast.173), kind=kCustom, calls=%fused_computation.2.clone.1 | custom fusion | flops 524288 | bytes 6291584 | tf_op jit(solution)/shard_map/vmap()/while/body/eval_jaxpr/scatter-add | solution.py:49
  226.3 2.1 reduce.10
  229.3 3.8 %all-to-all-start.4 = ((bf16[16,2,8192]{2,1,0:T(2,128)(2,1)}), bf16[16,2,8192]{2,1,0:T(2,128)(2,1)S(1)}, u32[]{:S(2)}, u32[]{:S(2)}) async-start(bf16[16,2,8192]{2,1,0:T(2,128)(2,1)} %reshape.252), calls=%async_computation.4 | async-start | bytes 1048576 | tf_op jit(solution)/shard_map/all_to_all | solution.py:109
  236.3 6.6 %all-to-all-done.4 = bf16[16,2,8192]{2,1,0:T(2,128)(2,1)S(1)} async-done(((bf16[16,2,8192]{2,1,0:T(2,128)(2,1)}), bf16[16,2,8192]{2,1,0:T(2,128)(2,1)S(1)}, u32[]{:S(2)}, u32[]{:S(2)}) %all-to-all-start.4) | async-done | bytes 524320 | tf_op jit(solution)/shard_map/all_to_all | solution.py:109
  243.0 3.6 %all-to-all-start.5 = ((bf16[16,2,8192]{2,1,0:T(2,128)(2,1)}), bf16[16,2,8192]{2,1,0:T(2,128)(2,1)S(1)}, u32[]{:S(2)}, u32[]{:S(2)}) async-start(bf16[16,2,8192]{2,1,0:T(2,128)(2,1)} %reshape.254), calls=%async_computation.5 | async-start | bytes 1048576 | tf_op jit(solution)/shard_map/all_to_all | solution.py:110
  249.8 6.0 %all-to-all-done.5 = bf16[16,2,8192]{2,1,0:T(2,128)(2,1)S(1)} async-done(((bf16[16,2,8192]{2,1,0:T(2,128)(2,1)}), bf16[16,2,8192]{2,1,0:T(2,128)(2,1)S(1)}, u32[]{:S(2)}, u32[]{:S(2)}) %all-to-all-start.5) | async-done | bytes 524320 | tf_op jit(solution)/shard_map/all_to_all | solution.py:110
  255.8 3.6 %all-to-all-start.6 = ((bf16[16,2,8192]{2,1,0:T(2,128)(2,1)}), bf16[16,2,8192]{2,1,0:T(2,128)(2,1)S(1)}, u32[]{:S(2)}, u32[]{:S(2)}) async-start(bf16[16,2,8192]{2,1,0:T(2,128)(2,1)} %reshape.256), calls=%async_computation.6 | async-start | bytes 1048576 | tf_op jit(solution)/shard_map/all_to_all | solution.py:111
  263.2 5.1 %all-to-all-done.6 = bf16[16,2,8192]{2,1,0:T(2,128)(2,1)S(1)} async-done(((bf16[16,2,8192]{2,1,0:T(2,128)(2,1)}), bf16[16,2,8192]{2,1,0:T(2,128)(2,1)S(1)}, u32[]{:S(2)}, u32[]{:S(2)}) %all-to-all-start.6) | async-done | bytes 524320 | tf_op jit(solution)/shard_map/all_to_all | solution.py:111
  (120 shorter events, 63.1 us)
Async XLA Ops:
  7.2 87.4 %copy-start = (bf16[1,128,2048]{2,1,0:T(8,128)(2,1)S(1)}, bf16[1,128,2048]{2,1,0:T(8,128)(2,1)}, u32[]{:S(2)}) copy-start(bf16[1,128,2048]{2,1,0:T(8,128)(2,1)} %param.12) | copy-start | bytes 1572868
  7.2 10.5 %copy-start.3 = (bf16[1,128,2048]{2,1,0:T(8,128)(2,1)S(1)}, bf16[1,128,2048]{2,1,0:T(8,128)(2,1)}, u32[]{:S(2)}) copy-start(bf16[1,128,2048]{2,1,0:T(8,128)(2,1)} %param.10) | copy-start | bytes 1572868
  7.2 87.4 %all-gather.2.cloned.1.call-start = ((), (), s32[]{:S(2)}) async-start(), calls=%async_computation.7 | async-start | bytes 8650752 | tf_op jit(solution)/shard_map/all_gather | solution.py:96
  9.1 21.2 %copy-start.4 = (bf16[1,128,2048]{2,1,0:T(8,128)(2,1)S(1)}, bf16[1,128,2048]{2,1,0:T(8,128)(2,1)}, u32[]{:S(2)}) copy-start(bf16[1,128,2048]{2,1,0:T(8,128)(2,1)} %param.11) | copy-start | bytes 1572868
  10.0 16.7 %all-to-all-start = ((bf16[128,16,128]{2,0,1:T(8,128)(2,1)}), bf16[128,16,128]{2,0,1:T(8,128)(2,1)}, u32[]{:S(2)}, u32[]{:S(2)}) async-start(bf16[128,16,128]{2,0,1:T(8,128)(2,1)} %copy.81), calls=%async_computation | async-start | bytes 1048576 | tf_op jit(solution)/shard_map/all_to_all | solution.py:86
  26.7 12.6 %all-to-all-start.1 = ((bf16[128,16,128]{0,2,1:T(8,128)(2,1)}), bf16[128,16,128]{0,2,1:T(8,128)(2,1)S(1)}, u32[]{:S(2)}, u32[]{:S(2)}) async-start(bf16[128,16,128]{0,2,1:T(8,128)(2,1)} %bitcast.29), calls=%async_computation.1 | async-start | bytes 1048576 | tf_op jit(solution)/shard_map/all_to_all | solution.py:87
  39.3 62.5 %all-to-all-start.3 = ((bf16[128,16,128]{0,2,1:T(8,128)(2,1)}), bf16[128,16,128]{0,2,1:T(8,128)(2,1)S(1)}, u32[]{:S(2)}, u32[]{:S(2)}) async-start(bf16[128,16,128]{0,2,1:T(8,128)(2,1)} %bitcast.38), calls=%async_computation.3 | async-start | bytes 1048576 | tf_op jit(solution)/shard_map/all_to_all | solution.py:88
  100.8 8.3 %copy-start.6 = (s32[1,16]{1,0:T(1,128)S(1)}, s32[1,16]{1,0:T(1,128)}, u32[]{:S(2)}) copy-start(s32[1,16]{1,0:T(1,128)} %param.15) | copy-start | bytes 196
  100.8 9.0 %copy-start.5 = (s32[1,16,8]{1,2,0:T(8,128)S(1)}, s32[1,16,8]{1,2,0:T(8,128)}, u32[]{:S(2)}) copy-start(s32[1,16,8]{1,2,0:T(8,128)} %param.14) | copy-start | bytes 1540
  101.8 17.6 %all-to-all-start.2 = ((bf16[128,16,128]{2,0,1:T(8,128)(2,1)}), bf16[128,16,128]{2,0,1:T(8,128)(2,1)}, u32[]{:S(2)}, u32[]{:S(2)}) async-start(bf16[128,16,128]{2,0,1:T(8,128)(2,1)} %bitcast.120), calls=%async_computation.2 | async-start | bytes 1048576 | tf_op jit(solution)/shard_map/all_to_all | solution.py:101
  125.4 2.1 copy-start.2
  131.1 2.8 %copy-start.1 = (bf16[4,128,8,128]{1,3,2,0:T(8,128)(2,1)}, bf16[4,128,8,128]{1,3,2,0:T(8,128)(2,1)S(1)}, u32[]{:S(2)}) copy-start(bf16[4,128,8,128]{1,3,2,0:T(8,128)(2,1)S(1)} %multiply_convert_fusion.3) | copy-start | bytes 3145732 | tf_op jit(solution)/shard_map/vmap()/while
  151.4 2.1 copy-start.2
  157.1 2.8 %copy-start.1 = (bf16[4,128,8,128]{1,3,2,0:T(8,128)(2,1)}, bf16[4,128,8,128]{1,3,2,0:T(8,128)(2,1)S(1)}, u32[]{:S(2)}) copy-start(bf16[4,128,8,128]{1,3,2,0:T(8,128)(2,1)S(1)} %multiply_convert_fusion.3) | copy-start | bytes 3145732 | tf_op jit(solution)/shard_map/vmap()/while
  177.5 2.1 copy-start.2
  183.1 2.8 %copy-start.1 = (bf16[4,128,8,128]{1,3,2,0:T(8,128)(2,1)}, bf16[4,128,8,128]{1,3,2,0:T(8,128)(2,1)S(1)}, u32[]{:S(2)}) copy-start(bf16[4,128,8,128]{1,3,2,0:T(8,128)(2,1)S(1)} %multiply_convert_fusion.3) | copy-start | bytes 3145732 | tf_op jit(solution)/shard_map/vmap()/while
  203.5 2.1 copy-start.2
  209.1 2.8 %copy-start.1 = (bf16[4,128,8,128]{1,3,2,0:T(8,128)(2,1)}, bf16[4,128,8,128]{1,3,2,0:T(8,128)(2,1)S(1)}, u32[]{:S(2)}) copy-start(bf16[4,128,8,128]{1,3,2,0:T(8,128)(2,1)S(1)} %multiply_convert_fusion.3) | copy-start | bytes 3145732 | tf_op jit(solution)/shard_map/vmap()/while
  229.3 13.7 %all-to-all-start.4 = ((bf16[16,2,8192]{2,1,0:T(2,128)(2,1)}), bf16[16,2,8192]{2,1,0:T(2,128)(2,1)S(1)}, u32[]{:S(2)}, u32[]{:S(2)}) async-start(bf16[16,2,8192]{2,1,0:T(2,128)(2,1)} %reshape.252), calls=%async_computation.4 | async-start | bytes 1048576 | tf_op jit(solution)/shard_map/all_to_all | solution.py:109
  243.0 12.9 %all-to-all-start.5 = ((bf16[16,2,8192]{2,1,0:T(2,128)(2,1)}), bf16[16,2,8192]{2,1,0:T(2,128)(2,1)S(1)}, u32[]{:S(2)}, u32[]{:S(2)}) async-start(bf16[16,2,8192]{2,1,0:T(2,128)(2,1)} %reshape.254), calls=%async_computation.5 | async-start | bytes 1048576 | tf_op jit(solution)/shard_map/all_to_all | solution.py:110
  255.8 12.5 %all-to-all-start.6 = ((bf16[16,2,8192]{2,1,0:T(2,128)(2,1)}), bf16[16,2,8192]{2,1,0:T(2,128)(2,1)S(1)}, u32[]{:S(2)}, u32[]{:S(2)}) async-start(bf16[16,2,8192]{2,1,0:T(2,128)(2,1)} %reshape.256), calls=%async_computation.6 | async-start | bytes 1048576 | tf_op jit(solution)/shard_map/all_to_all | solution.py:111
Sparse Core Ops, SparseCore 0:
  10.1 84.3 all-gather.1
where the time goes:
time: 282 us; the launch traced here: 277 us
  waiting for transfers between devices  94.4 us (33%)
  other arithmetic  59.1 us (21%)
  matrix products  43.9 us (16%)
  local copies, waits for them, and re-layouts  32.8 us (12%)
  starting transfers between devices  32.5 us (12%)
  between operations  14.3 us (5%)
    all_gather x1, waiting for transfers between devices, local(): lax.all_gather(out_weight, 'dp', axis=0, tiled=True)  51.7 us
    scatter-add x8, other arithmetic, scan_step(): key_sum = key_sum.at[lists_group].add(key_parts)  24.4 us
    scatter-add x4, other arithmetic, scan_step(): value_sum = value_sum.at[lists_group].add(value_parts)  24.4 us
    unnamed x27, local copies, waits for them, and re-layouts  11.3 us
    gather x4, local copies, waits for them, and re-layouts, scan_step(): value_sets = value_blocks[lists_group]  10.9 us
    all_to_all x1, waiting for transfers between devices, local(): lax.all_to_all(split_heads(attn_low), 'seq', split_axis=1, concat_axis=0,...  8.22 us
    all_to_all x1, waiting for transfers between devices, local(): lax.all_to_all(split_heads(queries), 'seq', split_axis=1, concat_axis=0,...  8.03 us
    all_to_all x1, waiting for transfers between devices, local(): lax.all_to_all(split_heads(key_states), 'seq', split_axis=1, concat_axis=...  7.96 us
  transfers between devices with their start and end apart: 8, of which 7 were waited for; matrix products, arithmetic and copies ran while one was open for 9% of the time, Pallas kernels for 0%

commit v1 on v0

v1 whole, which is shorter than its diff:
```python
import functools

import jax
import jax.numpy as jnp
from jax import lax
from jax.experimental import pallas as pl
from jax.experimental.pallas import tpu as pltpu
from jax.sharding import PartitionSpec as P

MESH = pl.DeviceIdType.MESH
HD = 128
NS = 16
NZ = 16
NBLK = 16
TOK = 128
HALF = HD // 2
PIECES = 2
PROWS = HALF // 2 // PIECES
FWD, BWD = 0, 1
HOPS = (NZ // 2, NZ // 2 - 1)
OFFSETS = (
    (1, 0), (3, 0), (0, 1), (0, 3), (1, 1), (3, 3), (1, 3), (3, 1),
    (2, 0), (0, 2), (2, 1), (2, 3), (1, 2), (3, 2), (2, 2),
)


def aligned(index, size):
    return pl.ds(pl.multiple_of(index * size, size), size)


def plane_peers(seq):
    y, x = seq // 4, seq % 4
    return [((y + dy) % 4) * 4 + (x + dx) % 4 for dx, dy in OFFSETS]


def enter(devices):
    barrier = pltpu.get_barrier_semaphore()
    for device in devices:
        pl.semaphore_signal(barrier, inc=1, device_id=device, device_id_type=MESH)
    pl.semaphore_wait(barrier, len(devices))


def remote(src, dst, send_sem, recv_sem, device):
    return pltpu.make_async_remote_copy(
        src_ref=src, dst_ref=dst, send_sem=send_sem, recv_sem=recv_sem,
        device_id=device, device_id_type=MESH,
    )


def weight_rows(hop, way):
    if hop == 0:
        return 0, 0
    if hop == NZ // 2:
        return 0, HALF
    return hop, way * HALF


def gather_kernel(
    q_in, k_in, v_in, g_in, w_in, q_out, k_out, v_out, gt_out,
    rows, weights, product,
    head_send, head_recv, head_local, row_send, row_recv, row_local,
    w_local, w_send0, own_send, own_recv, w_send, w_recv, core_send, core_recv,
    g_send, g_recv, g_local,
):
    seq, dp = lax.axis_index("seq"), lax.axis_index("dp")
    z, core = dp // 2, dp % 2
    side = seq % 2
    pair = seq + 1 - 2 * side
    partner = (seq, z * 2 + 1 - core)
    peers = plane_peers(seq)

    def along(way, c):
        step = 1 if way == FWD else NZ - 1
        return (seq, ((z + step) % NZ) * 2 + c)

    enter(
        [(p, dp) for p in peers]
        + [partner]
        + [along(way, c) for way in (FWD, BWD) for c in (0, 1)]
    )

    def first_copies():
        copies = []
        for piece in range(PIECES):
            for way in (FWD, BWD):
                slot, base = weight_rows(1, way)
                for c in (0, 1):
                    at = c * (HALF // 2) + piece * PROWS
                    copies.append(remote(
                        w_in.at[pl.ds(at, PROWS), :],
                        weights.at[slot, pl.ds(base + at, PROWS), :],
                        w_send0.at[way, c, piece], w_recv.at[way, 1, piece],
                        along(way, c),
                    ))
        copies.append(remote(
            w_in, weights.at[0, pl.ds(0, HALF), :], own_send, own_recv, partner
        ))
        return copies

    own_copy = pltpu.make_async_copy(w_in, weights.at[0, pl.ds(0, HALF), :], w_local)

    @pl.when(core == side)
    def _():
        for copy in first_copies():
            copy.start()
        own_copy.start()

    row_copy = remote(
        g_in, rows.at[aligned(side, TOK), :], row_send, row_recv, (pair, dp)
    )
    row_copy.start()
    row_here = pltpu.make_async_copy(g_in, rows.at[aligned(side, TOK), :], row_local)
    row_here.start()

    head_copies, head_here = [], []
    for n, (src, dst) in enumerate(((q_in, q_out), (k_in, k_out), (v_in, v_out))):
        copy = pltpu.make_async_copy(
            src.at[:, aligned(seq, HD)], dst.at[aligned(seq, TOK), :], head_local.at[n]
        )
        copy.start()
        head_here.append(copy)
        for m, p in enumerate(peers):
            copy = remote(
                src.at[:, aligned(p, HD)], dst.at[aligned(seq, TOK), :],
                head_send.at[n, m], head_recv.at[n, m], (p, dp),
            )
            copy.start()
            head_copies.append(copy)

    def quarter(hop, way, c, piece):
        slot, base = weight_rows(hop, way)
        at = base + piece * PROWS + c * (HALF // 2)
        return weights.at[slot, pl.ds(pl.multiple_of(at, PROWS), PROWS), :]

    def onward(hop, way, piece):
        return remote(
            quarter(hop, way, core, piece), quarter(hop + 1, way, core, piece),
            w_send.at[way, hop, piece], w_recv.at[way, hop + 1, piece],
            along(way, core),
        )

    def arrival(hop, way, piece):
        here = quarter(hop, way, core, piece)
        return remote(
            here, here, w_send.at[way, hop, piece], w_recv.at[way, hop, piece],
            along(way, core),
        )

    def across(hop, way, piece):
        here = quarter(hop, way, core, piece)
        return remote(
            here, here, core_send.at[way, hop, piece], core_recv.at[way, hop, piece],
            partner,
        )

    def head_send_copy(slot, way, owner):
        return remote(
            product.at[slot, pl.ds(way * HALF, HALF), :],
            gt_out.at[aligned(side, HALF), aligned(seq // 2, 2 * TOK)],
            g_send.at[slot, way], g_recv.at[seq], (owner, dp),
        )

    def head_local_copy(slot, way):
        return pltpu.make_async_copy(
            product.at[slot, pl.ds(way * HALF, HALF), :],
            gt_out.at[aligned(side, HALF), aligned(seq // 2, 2 * TOK)],
            g_local,
        )

    def owners(slot):
        if slot == 0:
            return z, (z + NZ // 2) % NZ
        return (z + NZ - slot) % NZ, (z + slot) % NZ

    def project(slot):
        product[slot] = lax.dot_general(
            weights[slot], rows[...], (((1,), (1,)), ((), ())),
            preferred_element_type=jnp.float32,
        ).astype(jnp.bfloat16)
        for way, owner in enumerate(owners(slot)):
            @pl.when(owner != seq)
            def _(way=way, owner=owner):
                head_send_copy(slot, way, owner).start()

            @pl.when(owner == seq)
            def _(way=way):
                head_local_copy(slot, way).start()

    for hop in range(1, NZ // 2 + 1):
        ways = [way for way in (FWD, BWD) if hop <= HOPS[way]]
        for piece in range(PIECES):
            for way in ways:
                arrival(hop, way, piece).wait_recv()
                if hop < HOPS[way]:
                    onward(hop, way, piece).start()
                across(hop, way, piece).start()
        if hop == 1:
            row_here.wait()
            row_copy.wait()
        else:
            for piece in range(PIECES):
                for way in (FWD, BWD):
                    across(hop - 1, way, piece).wait_recv()
            project(hop - 1)
    for piece in range(PIECES):
        across(NZ // 2, FWD, piece).wait_recv()

    @pl.when(core == side)
    def _():
        own_copy.wait()

    @pl.when(core != side)
    def _():
        remote(
            w_in, weights.at[0, pl.ds(0, HALF), :], own_send, own_recv, partner
        ).wait_recv()

    project(0)

    @pl.when(core == side)
    def _():
        for copy in first_copies():
            copy.wait_send()

    for hop in range(1, NZ // 2 + 1):
        for piece in range(PIECES):
            for way in (FWD, BWD):
                if hop < HOPS[way]:
                    onward(hop, way, piece).wait_send()
                if hop <= HOPS[way]:
                    across(hop, way, piece).wait_send()
    for copy in head_here:
        copy.wait()
    for copy in head_copies:
        copy.wait()
    for slot in range(NZ // 2):
        for way, owner in enumerate(owners(slot)):
            @pl.when(owner != seq)
            def _(slot=slot, way=way, owner=owner):
                head_send_copy(slot, way, owner).wait_send()

            @pl.when(owner == seq)
            def _(slot=slot, way=way):
                head_local_copy(slot, way).wait()
    for other in range(NS):
        @pl.when(other != seq)
        def _(other=other):
            block = gt_out.at[pl.ds(0, HALF), pl.ds(0, 2 * TOK)]
            remote(
                block, block, g_send.at[0, 0], g_recv.at[other], (other, dp)
            ).wait_recv()


def gather_heads(q, k, v, g, w):
    dma = pltpu.SemaphoreType.DMA
    heads = jax.ShapeDtypeStruct((NS * TOK, HD), jnp.bfloat16)
    turned = jax.ShapeDtypeStruct((HD, NS * TOK), jnp.bfloat16)
    width = g.shape[1]
    anywhere = pl.BlockSpec(memory_space=pl.ANY)
    hops = NZ // 2 + 1
    return pl.pallas_call(
        gather_kernel,
        name="gather_heads",
        out_shape=[heads, heads, heads, turned],
        in_specs=[anywhere] * 5,
        out_specs=[anywhere] * 4,
        scratch_shapes=[
            pltpu.VMEM((2 * TOK, width), jnp.bfloat16),
            pltpu.VMEM((NZ // 2, HD, width), jnp.bfloat16),
            pltpu.VMEM((NZ // 2, HD, 2 * TOK), jnp.bfloat16),
            dma((3, len(OFFSETS))), dma((3, len(OFFSETS))), dma((3,)),
            dma, dma, dma,
            dma, dma((2, 2, PIECES)), dma, dma,
            dma((2, hops, PIECES)), dma((2, hops, PIECES)),
            dma((2, hops, PIECES)), dma((2, hops, PIECES)),
            dma((NZ // 2, 2)), dma((NS,)), dma,
        ],
        compiler_params=pltpu.CompilerParams(
            collective_id=0, has_side_effects=True, vmem_limit_bytes=24 << 20
        ),
    )(q, k, v, g, w)


def attention_kernel(
    lists, counts, q, k, v, gt, dq, dk, dv, k_turned, score, prob_grad, dk_sum, dv_sum
):
    scale = HD ** -0.5
    exponent = scale * 1.4426950408889634
    dk_sum[...] = jnp.zeros_like(dk_sum)
    dv_sum[...] = jnp.zeros_like(dv_sum)
    for t in range(NBLK):
        k_turned[t] = k[pl.ds(t * TOK, TOK), :].T

    def fold(x, op):
        return op(x.reshape(TOK // 8, 8, TOK), axis=0)

    def query_block(i, carry):
        q_rows = q[aligned(i, TOK), :]
        g_cols = gt[:, aligned(i, TOK)]
        g_rows = g_cols.T

        def run(n):
            blocks = [lists[0, i, j] for j in range(n)]
            top = None
            for j, t in enumerate(blocks):
                s = lax.dot_general(
                    k[aligned(t, TOK), :], q_rows, (((1,), (1,)), ((), ())),
                    preferred_element_type=jnp.float32,
                )
                score[j] = s
                part = fold(s, jnp.max)
                top = part if top is None else jnp.maximum(top, part)
            top = jnp.max(top, axis=0, keepdims=True)
            total = delta = None
            for j, t in enumerate(blocks):
                weight = jnp.exp2((score[j] - top) * exponent)
                score[j] = weight
                d = jnp.dot(v[aligned(t, TOK), :], g_cols, preferred_element_type=jnp.float32)
                prob_grad[j] = d
                one, two = fold(weight, jnp.sum), fold(weight * d, jnp.sum)
                total = one if total is None else total + one
                delta = two if delta is None else delta + two
            inverse = 1.0 / jnp.sum(total, axis=0, keepdims=True)
            delta = jnp.sum(delta, axis=0, keepdims=True) * inverse
            q_sum = None
            for j, t in enumerate(blocks):
                probs = score[j] * inverse
                probs_low = probs.astype(jnp.bfloat16)
                score_low = (probs * (prob_grad[j] - delta)).astype(jnp.bfloat16)
                at = aligned(t, TOK)
                dv_sum[at, :] += jnp.dot(probs_low, g_rows, preferred_element_type=jnp.float32)
                dk_sum[at, :] += jnp.dot(score_low, q_rows, preferred_element_type=jnp.float32)
                part = jnp.dot(k_turned[t], score_low, preferred_element_type=jnp.float32)
                q_sum = part if q_sum is None else q_sum + part
            dq[aligned(i, TOK), :] = (q_sum.T * scale).astype(jnp.bfloat16)

        for n in range(1, 9):
            pl.when(counts[0, i] == n)(functools.partial(run, n))
        return carry

    lax.fori_loop(0, NBLK, query_block, 0)
    dk[...] = (dk_sum[...] * scale).astype(jnp.bfloat16)
    dv[...] = dv_sum[...].astype(jnp.bfloat16)


def attention_grads(lists, counts, q, k, v, gt):
    heads = jax.ShapeDtypeStruct((NBLK * TOK, HD), jnp.bfloat16)
    scalars = pl.BlockSpec(memory_space=pltpu.SMEM)
    whole = pl.BlockSpec(memory_space=pltpu.VMEM)
    return pl.pallas_call(
        attention_kernel,
        name="attention_grads",
        out_shape=[heads] * 3,
        in_specs=[scalars] * 2 + [whole] * 4,
        out_specs=[whole] * 3,
        scratch_shapes=[
            pltpu.VMEM((NBLK, HD, TOK), jnp.bfloat16),
            pltpu.VMEM((8, TOK, TOK), jnp.float32),
            pltpu.VMEM((8, TOK, TOK), jnp.float32),
            pltpu.VMEM((NBLK * TOK, HD), jnp.float32),
            pltpu.VMEM((NBLK * TOK, HD), jnp.float32),
        ],
        compiler_params=pltpu.CompilerParams(vmem_limit_bytes=24 << 20),
    )(lists, counts, q, k, v, gt)


def scatter_kernel(*refs):
    ins, outs = refs[:3], refs[3:6]
    send_sem, recv_sem, local_sem = refs[6:]
    seq, dp = lax.axis_index("seq"), lax.axis_index("dp")
    peers = plane_peers(seq)
    enter([(p, dp) for p in peers])
    copies = []
    for n, (src, dst) in enumerate(zip(ins, outs)):
        for m, p in enumerate(peers):
            copies.append(remote(
                src.at[aligned(p, TOK), :], dst.at[:, aligned(seq, HD)],
                send_sem.at[n, m], recv_sem.at[n, m], (p, dp),
            ))
            copies[-1].start()
    for n, (src, dst) in enumerate(zip(ins, outs)):
        copies.append(pltpu.make_async_copy(
            src.at[aligned(seq, TOK), :], dst.at[:, aligned(seq, HD)], local_sem.at[n]
        ))
        copies[-1].start()
    for copy in copies:
        copy.wait()


def scatter_heads(dq, dk, dv):
    dma = pltpu.SemaphoreType.DMA
    anywhere = pl.BlockSpec(memory_space=pl.ANY)
    return pl.pallas_call(
        scatter_kernel,
        name="scatter_heads",
        out_shape=[jax.ShapeDtypeStruct((TOK, NS * HD), jnp.bfloat16)] * 3,
        in_specs=[anywhere] * 3,
        out_specs=[anywhere] * 3,
        scratch_shapes=[dma((3, len(OFFSETS))), dma((3, len(OFFSETS))), dma((3,))],
        compiler_params=pltpu.CompilerParams(
            collective_id=1, has_side_effects=True, vmem_limit_bytes=24 << 20
        ),
    )(dq, dk, dv)


def local(queries, key_states, value_states, grad_out, out_weight, block_lists, block_counts):
    flat = [a.reshape(a.shape[1:]) for a in (queries, key_states, value_states, grad_out)]
    q, k, v, gt = gather_heads(*flat, out_weight)
    grads = attention_grads(block_lists, block_counts, q, k, v, gt)
    return tuple(out[None] for out in scatter_heads(*grads))


def solution(mesh):
    tokens = P("dp", "seq", None)
    return jax.shard_map(
        local,
        mesh=mesh,
        in_specs=(tokens,) * 4 + (P("dp", None), P("seq", None, None), P("seq", None)),
        out_specs=(tokens,) * 3,
        check_vma=False,
    )
```

time: 282 us -> 109 us (0.39); the launches traced: 277 us -> 108 us
  Pallas kernels: 0 us -> 98.6 us
  waiting for transfers between devices: 94.4 us -> 0 us
  other arithmetic: 59.1 us -> 0 us
  matrix products: 43.9 us -> 0 us
  starting transfers between devices: 32.5 us -> 0 us
  local copies, waits for them, and re-layouts: 32.8 us -> 8.9 us
  between operations: 14.3 us -> 0.68 us
    pallas_call x0 -> x3, Pallas kernels: none -> 98.6 us  [the longest x1 64.5 us: gather_heads(): pl.pallas_call(gather_kernel, name='gather_heads', out_shape=[heads, head...]
    all_gather x1 -> x0, waiting for transfers between devices: 51.7 us -> none  [local(): lax.all_gather(out_weight, 'dp', axis=0, tiled=True)]
    scatter-add x12 -> x0, other arithmetic: 48.8 us -> none  [the longest x8 24.4 us: scan_step(): key_sum = key_sum.at[lists_group].add(key_parts)]
    dot_general x25 -> x0, matrix products: 43.9 us -> none  [the longest x4 7.21 us: scan_step(): jnp.einsum('gqjk,gjkd->gqd', probs_low, value_sets, preferred_element_typ...]
    all_to_all x7 -> x0, waiting for transfers between devices: 42 us -> none  [the longest x1 8.22 us: local(): lax.all_to_all(split_heads(attn_low), 'seq', split_axis=1, concat_axis=0,...]
    all_to_all x7 -> x0, starting transfers between devices: 32.4 us -> none  [the longest x1 7.62 us: local(): lax.all_to_all(split_heads(queries), 'seq', split_axis=1, concat_axis=0,...]
    gather x8 -> x0, local copies, waits for them, and re-layouts: 13.9 us -> none  [the longest x4 10.9 us: scan_step(): value_sets = value_blocks[lists_group]]
    unnamed x27 -> x18, local copies, waits for them, and re-layouts: 11.3 us -> 8.9 us
  transfers between devices with their start and end apart: 8 -> 0, of which waited for: 7 -> 0; matrix products, arithmetic and copies ran while one was open for 9% -> 0% of each run, Pallas kernels for 0% -> 0%
where the time goes in v1:
time: 109 us; the launch traced here: 108 us
  Pallas kernels  98.6 us (90%)
  local copies, waits for them, and re-layouts  8.9 us (8%)
    pallas_call x1, Pallas kernels, gather_heads(): pl.pallas_call(gather_kernel, name='gather_heads', out_shape=[heads, head...  64.5 us
    pallas_call x1, Pallas kernels, scatter_heads(): pl.pallas_call(scatter_kernel, name='scatter_heads', out_shape=[jax.Shape...  23.8 us
    pallas_call x1, Pallas kernels, attention_grads(): pl.pallas_call(attention_kernel, name='attention_grads', out_shape=[heads...  10.3 us
    unnamed x18, local copies, waits for them, and re-layouts  8.9 us

profile of v1, /device:TPU:1, one launch (start us, length us, event | category | flops | bytes accessed | tf_op | source)
XLA Modules:
  0.0 108.2 jit_solution(11091119561158287152)
XLA Ops:
  0.6 0.0 copy-start.6
  0.6 0.7 copy-done.6
  1.3 0.1 copy.10.lists
  1.4 0.0 copy-start
  1.4 1.0 copy-done
  2.4 0.0 copy-start.1
  2.4 1.0 copy-done.1
  3.5 0.0 copy-start.2
  3.5 1.0 copy-done.2
  4.5 0.0 copy-start.3
  4.5 1.0 copy-done.3
  5.6 0.0 copy-start.4
  5.6 0.9 copy-done.4
  6.5 64.5 %gather_heads.1 = (bf16[2048,128]{1,0:T(8,128)(2,1)S(1)}, bf16[2048,128]{1,0:T(8,128)(2,1)S(1)}, bf16[2048,128]{1,0:T(8,128)(2,1)S(1)}, bf16[128,2048]{1,0:T(8,128)(2,1)S(1)}) custom-call(bf16[128,2048]{1,0:T(8,128)(2,1)S(1)} %bitcast.10, bf16[128,2048]{1,0:T(8,128)(2,1)S(1)} %bitcast.11, bf16[128,2048]{1,0:T(8,128)(2,1)S(1)} %bitcast.12, ...), custom_call_target="tpu_custom_call" | custom-call | tf_op jit(solution)/shard_map/gather_heads/pallas_call | solution.py:261
  71.0 0.0 copy-start.5
  71.0 0.6 copy-done.5
  71.6 10.3 %attention_grads.1 = (bf16[2048,128]{1,0:T(8,128)(2,1)S(1)}, bf16[2048,128]{1,0:T(8,128)(2,1)S(1)}, bf16[2048,128]{1,0:T(8,128)(2,1)S(1)}) custom-call(s32[1,16,8]{2,1,0:T(8,128)S(1)} %copy.10.lists, s32[1,16]{1,0:T(1,128)S(1)} %copy-done.5, bf16[2048,128]{1,0:T(8,128)(2,1)S(1)} %get-tuple-element.13.q, bf16[2048,128]{1,0:T(8,128)(2,1)S(1)} %get-tuple-element.14.k, ...), custom_call_target="tpu_custom_call" | custom-call | tf_op jit(solution)/shard_map/attention_grads/pallas_call | solution.py:350
  82.0 23.8 %scatter_heads.1 = (bf16[128,2048]{1,0:T(8,128)(2,1)S(1)}, bf16[128,2048]{1,0:T(8,128)(2,1)S(1)}, bf16[128,2048]{1,0:T(8,128)(2,1)S(1)}) custom-call(bf16[2048,128]{1,0:T(8,128)(2,1)S(1)} %get-tuple-element.17.refs_0_, bf16[2048,128]{1,0:T(8,128)(2,1)S(1)} %get-tuple-element.18.refs_1_, bf16[2048,128]{1,0:T(8,128)(2,1)S(1)} %get-tuple-element.19.refs_2_), custom_call_target="tpu_custom_call" | custom-call | tf_op jit(solution)/shard_map/scatter_heads/pallas_call | solution.py:393
  105.8 0.8 copy.14
  106.6 0.8 copy.15
  107.4 0.8 copy.16
Async XLA Ops:
  0.6 0.7 copy-start.6
  1.4 1.0 copy-start
  2.4 1.0 copy-start.1
  3.5 1.0 copy-start.2
  4.5 1.0 copy-start.3
  5.6 0.9 copy-start.4
  71.0 0.7 copy-start.5

commit v2 on v1

--- a/solution.py
+++ b/solution.py
@@ -12,11 +12,16 @@
 NS = 16
 NZ = 16
 NBLK = 16
+KMAX = 8
+PAIRS = 64
+UNROLL = 4
 TOK = 128
 HALF = HD // 2
 PIECES = 2
 PROWS = HALF // 2 // PIECES
 FWD, BWD = 0, 1
+PROJECTS = {4: (1,), 5: (2, 3), 6: (4, 5), 7: (6,), 8: (7,)}
+GATHER_VMEM = 24 << 20
 HOPS = (NZ // 2, NZ // 2 - 1)
 OFFSETS = (
     (1, 0), (3, 0), (0, 1), (0, 3), (1, 1), (3, 3), (1, 3), (3, 1),
@@ -172,12 +177,15 @@
             return z, (z + NZ // 2) % NZ
         return (z + NZ - slot) % NZ, (z + slot) % NZ
 
-    def project(slot):
-        product[slot] = lax.dot_general(
-            weights[slot], rows[...], (((1,), (1,)), ((), ())),
+    def project(slot, ways):
+        span = pl.ds(ways[0] * HALF, len(ways) * HALF)
+        product[slot, span, :] = lax.dot_general(
+            weights[slot, span, :], rows[...], (((1,), (1,)), ((), ())),
             preferred_element_type=jnp.float32,
         ).astype(jnp.bfloat16)
-        for way, owner in enumerate(owners(slot)):
+        for way in ways:
+            owner = owners(slot)[way]
+
             @pl.when(owner != seq)
             def _(way=way, owner=owner):
                 head_send_copy(slot, way, owner).start()
@@ -194,28 +202,29 @@
                 if hop < HOPS[way]:
                     onward(hop, way, piece).start()
                 across(hop, way, piece).start()
-        if hop == 1:
+        if hop == min(PROJECTS):
             row_here.wait()
-            row_copy.wait()
-        else:
+            row_copy.wait_recv()
+
+            @pl.when(core == side)
+            def _():
+                own_copy.wait()
+
+            @pl.when(core != side)
+            def _():
+                remote(
+                    w_in, weights.at[0, pl.ds(0, HALF), :], own_send, own_recv, partner
+                ).wait_recv()
+
+            project(0, (FWD,))
+        for slot in PROJECTS.get(hop, ()):
             for piece in range(PIECES):
                 for way in (FWD, BWD):
-                    across(hop - 1, way, piece).wait_recv()
-            project(hop - 1)
+                    across(slot, way, piece).wait_recv()
+            project(slot, (FWD, BWD))
     for piece in range(PIECES):
         across(NZ // 2, FWD, piece).wait_recv()
-
-    @pl.when(core == side)
-    def _():
-        own_copy.wait()
-
-    @pl.when(core != side)
-    def _():
-        remote(
-            w_in, weights.at[0, pl.ds(0, HALF), :], own_send, own_recv, partner
-        ).wait_recv()
-
-    project(0)
+    project(0, (BWD,))
 
     @pl.when(core == side)
     def _():
@@ -229,6 +238,7 @@
                     onward(hop, way, piece).wait_send()
                 if hop <= HOPS[way]:
                     across(hop, way, piece).wait_send()
+    row_copy.wait_send()
     for copy in head_here:
         copy.wait()
     for copy in head_copies:
@@ -276,77 +286,102 @@
             dma((NZ // 2, 2)), dma((NS,)), dma,
         ],
         compiler_params=pltpu.CompilerParams(
-            collective_id=0, has_side_effects=True, vmem_limit_bytes=24 << 20
+            collective_id=0, has_side_effects=True, vmem_limit_bytes=GATHER_VMEM
         ),
     )(q, k, v, g, w)
 
 
 def attention_kernel(
-    lists, counts, q, k, v, gt, dq, dk, dv, k_turned, score, prob_grad, dk_sum, dv_sum
+    lists, counts, q, k, v, gt, dq, dk, dv,
+    pair_q, pair_k, k_turned, g_rows, score, prob_grad, top, total, delta,
+    dq_sum, dk_sum, dv_sum,
 ):
     scale = HD ** -0.5
     exponent = scale * 1.4426950408889634
+
+    used = jnp.int32(0)
+    for i in range(NBLK):
+        for j in range(KMAX):
+            pair_q[used + j] = jnp.int32(i)
+            pair_k[used + j] = lists[0, j, i]
+        used = used + counts[0, i]
+    steps = (used + UNROLL - 1) // UNROLL
+
     dk_sum[...] = jnp.zeros_like(dk_sum)
     dv_sum[...] = jnp.zeros_like(dv_sum)
+    dq_sum[...] = jnp.zeros_like(dq_sum)
+    top[...] = jnp.full_like(top, -1e30)
+    total[...] = jnp.zeros_like(total)
+    delta[...] = jnp.zeros_like(delta)
     for t in range(NBLK):
         k_turned[t] = k[pl.ds(t * TOK, TOK), :].T
-
-    def fold(x, op):
-        return op(x.reshape(TOK // 8, 8, TOK), axis=0)
-
-    def query_block(i, carry):
-        q_rows = q[aligned(i, TOK), :]
-        g_cols = gt[:, aligned(i, TOK)]
-        g_rows = g_cols.T
-
-        def run(n):
-            blocks = [lists[0, i, j] for j in range(n)]
-            top = None
-            for j, t in enumerate(blocks):
-                s = lax.dot_general(
-                    k[aligned(t, TOK), :], q_rows, (((1,), (1,)), ((), ())),
-                    preferred_element_type=jnp.float32,
-                )
-                score[j] = s
-                part = fold(s, jnp.max)
-                top = part if top is None else jnp.maximum(top, part)
-            top = jnp.max(top, axis=0, keepdims=True)
-            total = delta = None
-            for j, t in enumerate(blocks):
-                weight = jnp.exp2((score[j] - top) * exponent)
-                score[j] = weight
-                d = jnp.dot(v[aligned(t, TOK), :], g_cols, preferred_element_type=jnp.float32)
-                prob_grad[j] = d
-                one, two = fold(weight, jnp.sum), fold(weight * d, jnp.sum)
-                total = one if total is None else total + one
-                delta = two if delta is None else delta + two
-            inverse = 1.0 / jnp.sum(total, axis=0, keepdims=True)
-            delta = jnp.sum(delta, axis=0, keepdims=True) * inverse
-            q_sum = None
-            for j, t in enumerate(blocks):
-                probs = score[j] * inverse
-                probs_low = probs.astype(jnp.bfloat16)
-                score_low = (probs * (prob_grad[j] - delta)).astype(jnp.bfloat16)
-                at = aligned(t, TOK)
-                dv_sum[at, :] += jnp.dot(probs_low, g_rows, preferred_element_type=jnp.float32)
-                dk_sum[at, :] += jnp.dot(score_low, q_rows, preferred_element_type=jnp.float32)
-                part = jnp.dot(k_turned[t], score_low, preferred_element_type=jnp.float32)
-                q_sum = part if q_sum is None else q_sum + part
-            dq[aligned(i, TOK), :] = (q_sum.T * scale).astype(jnp.bfloat16)
-
-        for n in range(1, 9):
-            pl.when(counts[0, i] == n)(functools.partial(run, n))
-        return carry
-
-    lax.fori_loop(0, NBLK, query_block, 0)
-    dk[...] = (dk_sum[...] * scale).astype(jnp.bfloat16)
-    dv[...] = dv_sum[...].astype(jnp.bfloat16)
+        g_rows[t] = gt[:, pl.ds(t * TOK, TOK)].T
+
+    def tiles(x):
+        return x.reshape(TOK // 8, 8, TOK)
+
+    def each_pair(body):
+        def step(n, carry):
+            for m in range(UNROLL):
+                t = n * UNROLL + m
+                body(t, pair_q[t], pair_k[t])
+            return carry
+
+        lax.fori_loop(0, steps, step, 0)
+
+    def scores(t, i, b):
+        s = lax.dot_general(
+            k[aligned(b, TOK), :], q[aligned(i, TOK), :], (((1,), (1,)), ((), ())),
+            preferred_element_type=jnp.float32,
+        )
+        s = tiles(s) + jnp.where(t < used, 0.0, -1e30)
+        score[t] = s
+        top[i] = jnp.maximum(top[i], jnp.max(s, axis=0))
+        prob_grad[t] = tiles(jnp.dot(
+            v[aligned(b, TOK), :], gt[:, aligned(i, TOK)], preferred_element_type=jnp.float32
+        ))
+
+    each_pair(scores)
+    top[...] = jnp.broadcast_to(
+        jnp.max(top[...], axis=1, keepdims=True) * exponent, top.shape
+    )
+
+    def weigh(t, i, b):
+        weight = jnp.exp2(score[t] * exponent - top[i])
+        score[t] = weight
+        total[i] += jnp.sum(weight, axis=0)
+        delta[i] += jnp.sum(weight * prob_grad[t], axis=0)
+
+    each_pair(weigh)
+    inverse = 1.0 / jnp.sum(total[...], axis=1, keepdims=True)
+    delta[...] = jnp.broadcast_to(
+        jnp.sum(delta[...], axis=1, keepdims=True) * inverse, delta.shape
+    )
+    total[...] = jnp.broadcast_to(inverse, total.shape)
+
+    def gradients(t, i, b):
+        probs = score[t] * total[i]
+        probs_low = probs.reshape(TOK, TOK).astype(jnp.bfloat16)
+        score_low = (probs * (prob_grad[t] - delta[i])).reshape(TOK, TOK).astype(jnp.bfloat16)
+        dv_sum[b] += jnp.dot(probs_low, g_rows[i], preferred_element_type=jnp.float32)
+        dk_sum[b] += jnp.dot(
+            score_low, q[aligned(i, TOK), :], preferred_element_type=jnp.float32
+        )
+        dq_sum[i] += jnp.dot(k_turned[b], score_low, preferred_element_type=jnp.float32)
+
+    each_pair(gradients)
+    for t in range(NBLK):
+        rows = pl.ds(t * TOK, TOK)
+        dq[rows, :] = (dq_sum[t].T * scale).astype(jnp.bfloat16)
+        dk[rows, :] = (dk_sum[t] * scale).astype(jnp.bfloat16)
+        dv[rows, :] = dv_sum[t].astype(jnp.bfloat16)
 
 
 def attention_grads(lists, counts, q, k, v, gt):
     heads = jax.ShapeDtypeStruct((NBLK * TOK, HD), jnp.bfloat16)
     scalars = pl.BlockSpec(memory_space=pltpu.SMEM)
     whole = pl.BlockSpec(memory_space=pltpu.VMEM)
+    blocks = (NBLK, TOK, HD)
     return pl.pallas_call(
         attention_kernel,
         name="attention_grads",
@@ -354,13 +389,20 @@
         in_specs=[scalars] * 2 + [whole] * 4,
         out_specs=[whole] * 3,
         scratch_shapes=[
-            pltpu.VMEM((NBLK, HD, TOK), jnp.bfloat16),
-            pltpu.VMEM((8, TOK, TOK), jnp.float32),
-            pltpu.VMEM((8, TOK, TOK), jnp.float32),
-            pltpu.VMEM((NBLK * TOK, HD), jnp.float32),
-            pltpu.VMEM((NBLK * TOK, HD), jnp.float32),
+            pltpu.SMEM((PAIRS + KMAX,), jnp.int32),
+            pltpu.SMEM((PAIRS + KMAX,), jnp.int32),
+            pltpu.VMEM(blocks, jnp.bfloat16),
+            pltpu.VMEM(blocks, jnp.bfloat16),
+            pltpu.VMEM((PAIRS, TOK // 8, 8, TOK), jnp.float32),
+            pltpu.VMEM((PAIRS, TOK // 8, 8, TOK), jnp.float32),
+            pltpu.VMEM((NBLK, 8, TOK), jnp.float32),
+            pltpu.VMEM((NBLK, 8, TOK), jnp.float32),
+            pltpu.VMEM((NBLK, 8, TOK), jnp.float32),
+            pltpu.VMEM(blocks, jnp.float32),
+            pltpu.VMEM(blocks, jnp.float32),
+            pltpu.VMEM(blocks, jnp.float32),
         ],
-        compiler_params=pltpu.CompilerParams(vmem_limit_bytes=24 << 20),
+        compiler_params=pltpu.CompilerParams(vmem_limit_bytes=32 << 20),
     )(lists, counts, q, k, v, gt)
 
 
@@ -403,11 +445,36 @@
     )(dq, dk, dv)
 
 
+def store_kernel(*refs):
+    copies = [
+        pltpu.make_async_copy(src, dst, refs[6].at[n])
+        for n, (src, dst) in enumerate(zip(refs[:3], refs[3:6]))
+    ]
+    for copy in copies:
+        copy.start()
+    for copy in copies:
+        copy.wait()
+
+
+def store_results(*arrays):
+    anywhere = pl.BlockSpec(memory_space=pl.ANY)
+    return pl.pallas_call(
+        store_kernel,
+        name="store_results",
+        out_shape=[jax.ShapeDtypeStruct(a.shape, a.dtype) for a in arrays],
+        in_specs=[anywhere] * 3,
+        out_specs=[anywhere] * 3,
+        scratch_shapes=[pltpu.SemaphoreType.DMA((3,))],
+        compiler_params=pltpu.CompilerParams(vmem_limit_bytes=24 << 20),
+    )(*arrays)
+
+
 def local(queries, key_states, value_states, grad_out, out_weight, block_lists, block_counts):
     flat = [a.reshape(a.shape[1:]) for a in (queries, key_states, value_states, grad_out)]
-    q, k, v, gt = gather_heads(*flat, out_weight)
-    grads = attention_grads(block_lists, block_counts, q, k, v, gt)
-    return tuple(out[None] for out in scatter_heads(*grads))
+    held = [pltpu.with_memory_space_constraint(a, pltpu.HBM) for a in (*flat, out_weight)]
+    q, k, v, gt = gather_heads(*held)
+    grads = attention_grads(jnp.swapaxes(block_lists, 1, 2), block_counts, q, k, v, gt)
+    return tuple(out[None] for out in store_results(*scatter_heads(*grads)))
 
 
 def solution(mesh):

time: 109 us -> 90.2 us (0.83)
  Pallas kernels: 98.6 us -> 87.2 us
  local copies, waits for them, and re-layouts: 8.9 us -> 0.68 us
    pallas_call x1, Pallas kernels: 64.5 us -> 55.3 us  [gather_heads(): pl.pallas_call(gather_kernel, name='gather_heads', out_shape=[heads, head...]
    unnamed x18 -> x4, local copies, waits for them, and re-layouts: 8.9 us -> 0.68 us
    pallas_call x1, Pallas kernels: 10.3 us -> 6.3 us  [attention_grads(): pl.pallas_call(attention_kernel, name='attention_grads', out_shape=[heads...]
    pallas_call x0 -> x1, Pallas kernels: none -> 1.17 us  [store_results(): pl.pallas_call(store_kernel, name='store_results', out_shape=[jax.ShapeDt...]
where the time goes in v2:
time: 90.2 us; the launch traced here: 88.5 us
  Pallas kernels  87.2 us (97%)
    pallas_call x1, Pallas kernels, gather_heads(): pl.pallas_call(gather_kernel, name='gather_heads', out_shape=[heads, head...  55.3 us
    pallas_call x1, Pallas kernels, scatter_heads(): pl.pallas_call(scatter_kernel, name='scatter_heads', out_shape=[jax.Shape...  24.4 us
    pallas_call x1, Pallas kernels, attention_grads(): pl.pallas_call(attention_kernel, name='attention_grads', out_shape=[heads...  6.3 us

profile of v2, /device:TPU:1, one launch (start us, length us, event | category | flops | bytes accessed | tf_op | source)
XLA Modules:
  0.0 88.5 jit_solution(11250039789027855050)
XLA Ops:
  0.6 55.3 %gather_heads.1 = (bf16[2048,128]{1,0:T(8,128)(2,1)S(1)}, bf16[2048,128]{1,0:T(8,128)(2,1)S(1)}, bf16[2048,128]{1,0:T(8,128)(2,1)S(1)}, bf16[128,2048]{1,0:T(8,128)(2,1)S(1)}) custom-call(bf16[128,2048]{1,0:T(8,128)(2,1)} %bitcast.9, bf16[128,2048]{1,0:T(8,128)(2,1)} %bitcast.10, bf16[128,2048]{1,0:T(8,128)(2,1)} %bitcast.11, bf16[128,2048]{1,0:T(8,128)(2,1)} %bitcast.12, ...), custom_call_target="tpu_custom_call" | custom-call | tf_op jit(solution)/shard_map/gather_heads/pallas_call | solution.py:271
  56.0 0.0 copy-start
  56.0 0.0 copy-start.1
  56.0 0.7 copy-done
  56.6 0.0 copy-done.1
  56.6 6.3 %attention_grads.1 = (bf16[2048,128]{1,0:T(8,128)(2,1)S(1)}, bf16[2048,128]{1,0:T(8,128)(2,1)S(1)}, bf16[2048,128]{1,0:T(8,128)(2,1)S(1)}) custom-call(s32[1,8,16]{2,1,0:T(8,128)S(1)} %bitcast.8, s32[1,16]{1,0:T(1,128)S(1)} %copy-done.1, bf16[2048,128]{1,0:T(8,128)(2,1)S(1)} %get-tuple-element.16.q, bf16[2048,128]{1,0:T(8,128)(2,1)S(1)} %get-tuple-element.17.k, ...), custom_call_target="tpu_custom_call" | custom-call | tf_op jit(solution)/shard_map/attention_grads/pallas_call | solution.py:385
  63.0 24.4 %scatter_heads.1 = (bf16[128,2048]{1,0:T(8,128)(2,1)S(1)}, bf16[128,2048]{1,0:T(8,128)(2,1)S(1)}, bf16[128,2048]{1,0:T(8,128)(2,1)S(1)}) custom-call(bf16[2048,128]{1,0:T(8,128)(2,1)S(1)} %get-tuple-element.20.refs_0_, bf16[2048,128]{1,0:T(8,128)(2,1)S(1)} %get-tuple-element.21.refs_1_, bf16[2048,128]{1,0:T(8,128)(2,1)S(1)} %get-tuple-element.22.refs_2_), custom_call_target="tpu_custom_call" | custom-call | tf_op jit(solution)/shard_map/scatter_heads/pallas_call | solution.py:435
  87.4 1.2 %store_results.1 = (bf16[128,2048]{1,0:T(8,128)(2,1)}, bf16[128,2048]{1,0:T(8,128)(2,1)}, bf16[128,2048]{1,0:T(8,128)(2,1)}) custom-call(bf16[128,2048]{1,0:T(8,128)(2,1)S(1)} %get-tuple-element.23.refs_0_, bf16[128,2048]{1,0:T(8,128)(2,1)S(1)} %get-tuple-element.24.refs_1_, bf16[128,2048]{1,0:T(8,128)(2,1)S(1)} %get-tuple-element.25.refs_2_), custom_call_target="tpu_custom_call" | custom-call | tf_op jit(solution)/shard_map/store_results/pallas_call | solution.py:461
Async XLA Ops:
  56.0 0.7 copy-start
  56.0 0.7 copy-start.1

commit v3 on v2

--- a/solution.py
+++ b/solution.py
@@ -14,7 +14,7 @@
 NBLK = 16
 KMAX = 8
 PAIRS = 64
-UNROLL = 4
+UNROLL = 32
 TOK = 128
 HALF = HD // 2
 PIECES = 2
@@ -305,6 +305,9 @@
             pair_q[used + j] = jnp.int32(i)
             pair_k[used + j] = lists[0, j, i]
         used = used + counts[0, i]
+    for m in range(UNROLL):
+        pair_q[used + m] = jnp.int32(0)
+        pair_k[used + m] = jnp.int32(0)
     steps = (used + UNROLL - 1) // UNROLL
 
     dk_sum[...] = jnp.zeros_like(dk_sum)
@@ -389,8 +392,8 @@
         in_specs=[scalars] * 2 + [whole] * 4,
         out_specs=[whole] * 3,
         scratch_shapes=[
-            pltpu.SMEM((PAIRS + KMAX,), jnp.int32),
-            pltpu.SMEM((PAIRS + KMAX,), jnp.int32),
+            pltpu.SMEM((PAIRS + KMAX + UNROLL,), jnp.int32),
+            pltpu.SMEM((PAIRS + KMAX + UNROLL,), jnp.int32),
             pltpu.VMEM(blocks, jnp.bfloat16),
             pltpu.VMEM(blocks, jnp.bfloat16),
             pltpu.VMEM((PAIRS, TOK // 8, 8, TOK), jnp.float32),
@@ -473,7 +476,9 @@
     flat = [a.reshape(a.shape[1:]) for a in (queries, key_states, value_states, grad_out)]
     held = [pltpu.with_memory_space_constraint(a, pltpu.HBM) for a in (*flat, out_weight)]
     q, k, v, gt = gather_heads(*held)
-    grads = attention_grads(jnp.swapaxes(block_lists, 1, 2), block_counts, q, k, v, gt)
+    block_lists = pltpu.with_memory_space_constraint(jnp.swapaxes(block_lists, 1, 2), pltpu.HBM)
+    block_counts = pltpu.with_memory_space_constraint(block_counts, pltpu.HBM)
+    grads = attention_grads(block_lists, block_counts, q, k, v, gt)
     return tuple(out[None] for out in store_results(*scatter_heads(*grads)))
 
 

time: 90.2 us -> 88.5 us (0.981)
    pallas_call x1, Pallas kernels: 6.3 us -> 4.21 us  [attention_grads(): pl.pallas_call(attention_kernel, name='attention_grads', out_shape=[heads...]
    pallas_call x1, Pallas kernels: 24.4 us -> 25.8 us  [scatter_heads(): pl.pallas_call(scatter_kernel, name='scatter_heads', out_shape=[jax.Shape...]
where the time goes in v3:
time: 88.5 us; the launch traced here: 87.2 us
  Pallas kernels  86.5 us (98%)
    pallas_call x1, Pallas kernels, gather_heads(): pl.pallas_call(gather_kernel, name='gather_heads', out_shape=[heads, head...  55.3 us
    pallas_call x1, Pallas kernels, scatter_heads(): pl.pallas_call(scatter_kernel, name='scatter_heads', out_shape=[jax.Shape...  25.8 us
    pallas_call x1, Pallas kernels, attention_grads(): pl.pallas_call(attention_kernel, name='attention_grads', out_shape=[heads...  4.21 us

profile of v3, /device:TPU:1, one launch (start us, length us, event | category | flops | bytes accessed | tf_op | source)
XLA Modules:
  0.0 87.2 jit_solution(6042232305268856370)
XLA Ops:
  0.6 55.3 %gather_heads.1 = (bf16[2048,128]{1,0:T(8,128)(2,1)S(1)}, bf16[2048,128]{1,0:T(8,128)(2,1)S(1)}, bf16[2048,128]{1,0:T(8,128)(2,1)S(1)}, bf16[128,2048]{1,0:T(8,128)(2,1)S(1)}) custom-call(bf16[128,2048]{1,0:T(8,128)(2,1)} %bitcast.8, bf16[128,2048]{1,0:T(8,128)(2,1)} %bitcast.9, bf16[128,2048]{1,0:T(8,128)(2,1)} %bitcast.10, bf16[128,2048]{1,0:T(8,128)(2,1)} %bitcast.11, ...), custom_call_target="tpu_custom_call" | custom-call | tf_op jit(solution)/shard_map/gather_heads/pallas_call | solution.py:271
  56.0 4.2 %attention_grads.1 = (bf16[2048,128]{1,0:T(8,128)(2,1)S(1)}, bf16[2048,128]{1,0:T(8,128)(2,1)S(1)}, bf16[2048,128]{1,0:T(8,128)(2,1)S(1)}) custom-call(s32[1,8,16]{2,1,0:T(8,128)} %bitcast.12, s32[1,16]{1,0:T(1,128)} %counts.1, bf16[2048,128]{1,0:T(8,128)(2,1)S(1)} %get-tuple-element.16.q, bf16[2048,128]{1,0:T(8,128)(2,1)S(1)} %get-tuple-element.17.k, ...), custom_call_target="tpu_custom_call" | custom-call | tf_op jit(solution)/shard_map/attention_grads/pallas_call | solution.py:388
  60.2 25.8 %scatter_heads.1 = (bf16[128,2048]{1,0:T(8,128)(2,1)S(1)}, bf16[128,2048]{1,0:T(8,128)(2,1)S(1)}, bf16[128,2048]{1,0:T(8,128)(2,1)S(1)}) custom-call(bf16[2048,128]{1,0:T(8,128)(2,1)S(1)} %get-tuple-element.20.refs_0_, bf16[2048,128]{1,0:T(8,128)(2,1)S(1)} %get-tuple-element.21.refs_1_, bf16[2048,128]{1,0:T(8,128)(2,1)S(1)} %get-tuple-element.22.refs_2_), custom_call_target="tpu_custom_call" | custom-call | tf_op jit(solution)/shard_map/scatter_heads/pallas_call | solution.py:438
  86.0 1.2 %store_results.1 = (bf16[128,2048]{1,0:T(8,128)(2,1)}, bf16[128,2048]{1,0:T(8,128)(2,1)}, bf16[128,2048]{1,0:T(8,128)(2,1)}) custom-call(bf16[128,2048]{1,0:T(8,128)(2,1)S(1)} %get-tuple-element.23.refs_0_, bf16[128,2048]{1,0:T(8,128)(2,1)S(1)} %get-tuple-element.24.refs_1_, bf16[128,2048]{1,0:T(8,128)(2,1)S(1)} %get-tuple-element.25.refs_2_), custom_call_target="tpu_custom_call" | custom-call | tf_op jit(solution)/shard_map/store_results/pallas_call | solution.py:464

commit v4 on v3

--- a/solution.py
+++ b/solution.py
@@ -417,7 +417,7 @@
     enter([(p, dp) for p in peers])
     copies = []
     for n, (src, dst) in enumerate(zip(ins, outs)):
-        for m, p in enumerate(peers):
+        for m, p in reversed(list(enumerate(peers))):
             copies.append(remote(
                 src.at[aligned(p, TOK), :], dst.at[:, aligned(seq, HD)],
                 send_sem.at[n, m], recv_sem.at[n, m], (p, dp),

time: 88.5 us -> 88.9 us (level)
  no operation moved by 1% of the time
where the time goes in v4:
time: 88.9 us; the launch traced here: 87.3 us
  Pallas kernels  86.7 us (98%)
    pallas_call x1, Pallas kernels, gather_heads(): pl.pallas_call(gather_kernel, name='gather_heads', out_shape=[heads, head...  55.3 us
    pallas_call x1, Pallas kernels, scatter_heads(): pl.pallas_call(scatter_kernel, name='scatter_heads', out_shape=[jax.Shape...  26 us
    pallas_call x1, Pallas kernels, attention_grads(): pl.pallas_call(attention_kernel, name='attention_grads', out_shape=[heads...  4.2 us

profile of v4, /device:TPU:1, one launch (start us, length us, event | category | flops | bytes accessed | tf_op | source)
XLA Modules:
  0.0 87.3 jit_solution(2839753469364199570)
XLA Ops:
  0.6 55.3 %gather_heads.1 = (bf16[2048,128]{1,0:T(8,128)(2,1)S(1)}, bf16[2048,128]{1,0:T(8,128)(2,1)S(1)}, bf16[2048,128]{1,0:T(8,128)(2,1)S(1)}, bf16[128,2048]{1,0:T(8,128)(2,1)S(1)}) custom-call(bf16[128,2048]{1,0:T(8,128)(2,1)} %bitcast.8, bf16[128,2048]{1,0:T(8,128)(2,1)} %bitcast.9, bf16[128,2048]{1,0:T(8,128)(2,1)} %bitcast.10, bf16[128,2048]{1,0:T(8,128)(2,1)} %bitcast.11, ...), custom_call_target="tpu_custom_call" | custom-call | tf_op jit(solution)/shard_map/gather_heads/pallas_call | solution.py:271
  56.0 4.2 %attention_grads.1 = (bf16[2048,128]{1,0:T(8,128)(2,1)S(1)}, bf16[2048,128]{1,0:T(8,128)(2,1)S(1)}, bf16[2048,128]{1,0:T(8,128)(2,1)S(1)}) custom-call(s32[1,8,16]{2,1,0:T(8,128)} %bitcast.12, s32[1,16]{1,0:T(1,128)} %counts.1, bf16[2048,128]{1,0:T(8,128)(2,1)S(1)} %get-tuple-element.16.q, bf16[2048,128]{1,0:T(8,128)(2,1)S(1)} %get-tuple-element.17.k, ...), custom_call_target="tpu_custom_call" | custom-call | tf_op jit(solution)/shard_map/attention_grads/pallas_call | solution.py:388
  60.2 26.0 %scatter_heads.1 = (bf16[128,2048]{1,0:T(8,128)(2,1)S(1)}, bf16[128,2048]{1,0:T(8,128)(2,1)S(1)}, bf16[128,2048]{1,0:T(8,128)(2,1)S(1)}) custom-call(bf16[2048,128]{1,0:T(8,128)(2,1)S(1)} %get-tuple-element.20.refs_0_, bf16[2048,128]{1,0:T(8,128)(2,1)S(1)} %get-tuple-element.21.refs_1_, bf16[2048,128]{1,0:T(8,128)(2,1)S(1)} %get-tuple-element.22.refs_2_), custom_call_target="tpu_custom_call" | custom-call | tf_op jit(solution)/shard_map/scatter_heads/pallas_call | solution.py:438
  86.1 1.2 %store_results.1 = (bf16[128,2048]{1,0:T(8,128)(2,1)}, bf16[128,2048]{1,0:T(8,128)(2,1)}, bf16[128,2048]{1,0:T(8,128)(2,1)}) custom-call(bf16[128,2048]{1,0:T(8,128)(2,1)S(1)} %get-tuple-element.23.refs_0_, bf16[128,2048]{1,0:T(8,128)(2,1)S(1)} %get-tuple-element.24.refs_1_, bf16[128,2048]{1,0:T(8,128)(2,1)S(1)} %get-tuple-element.25.refs_2_), custom_call_target="tpu_custom_call" | custom-call | tf_op jit(solution)/shard_map/store_results/pallas_call | solution.py:464
